TPU v7x, 1024 devices: a whole 4x4x32 slice. The times are simulated.
1024 devices in a mesh: section: 16 (over y, x_hi, core), fsdp: 32 (over z), tp: 2 (over x_lo).
Axes of the slice: x: 4 (x_hi: 2, x_lo: 2; x = x_hi * 2 + x_lo), y: 4, z: 32, core: 2. Of those that a mesh axis runs over, the one named last changes fastest.
Arguments:
- text_tokens: bfloat16 [65536, 8192], P(('section', 'fsdp')), may hold values from -45 to 45
- images: bfloat16 [256, 256, 8192], P('section', None, ('fsdp', 'tp')), may hold values from -45 to 45
- counts: int32 [256], P('section'), may hold values from 1 to 256, as said below
- offsets: int32 [256], P('section'), may hold values from 0 to 65535, as said below
- norm_gain: float32 [8192], replicated, may hold values from 0.25 to 1.75
- value_weight: bfloat16 [8192, 512], P(('fsdp', 'tp'), 'section'), may hold values from -0.0625 to 0.0625
- value_grad: bfloat16 [65536, 512], P(('section', 'fsdp')), may hold values from -6 to 6
Outputs:
- values: bfloat16 [65536, 512], P(('section', 'fsdp'), 'tp')
- visual_grads: bfloat16 [256, 256, 8192], P('section', None, ('fsdp', 'tp'))
Inputs may be any that keep to these rules, and one draw needn't show every extreme that they name: `counts`: on every section index some tile has exactly 256 visual tokens. Tile i occupies positions offsets[i] to offsets[i] + counts[i] - 1, all inside one aligned block of 256 positions. The positions of one section index form 16 such blocks. The 16 tiles of one section index go to 16 different section indices, and every block receives exactly one tile.
All inputs are finite; a program needn't handle non-finite values.
Results may differ from a plain program's by a relative error of at most 0.0049.
Values may be sent and summed in bfloat16 or wider, within the bound.
No kernel may reach another device: no remote copies, remote signals or barrier semaphores. Data moves between devices by JAX's collectives and lax.ppermute only.
A program may use at most 64 MiB of HBM per device.

v0:
```python
import jax
import jax.numpy as jnp
from jax import lax
from jax.sharding import PartitionSpec as P

epsilon = 1e-05


def joined_along(blocks, dim):
    dims = list(blocks.shape[1:])
    dims[dim] *= blocks.shape[0]
    return jnp.moveaxis(blocks, 0, dim).reshape(dims)


def sent_to_all(x, axis):
    copies = jnp.broadcast_to(x, (lax.axis_size(axis), *x.shape))
    return lax.all_to_all(copies, axis, split_axis=0, concat_axis=0, tiled=True)


def collect(x, axis, dim):
    return joined_along(sent_to_all(x, axis), dim)


def split_up(x, dim, length):
    before, after = (x.shape[:dim], x.shape[dim + 1 :])
    return jnp.moveaxis(x.reshape(*before, length, -1, *after), dim, 0)


def sent_and_summed(x, axis, dim):
    length = lax.axis_size(axis)
    blocks = lax.all_to_all(split_up(x, dim, length), axis, 0, 0, tiled=True)
    return jnp.sum(blocks, axis=0)


def on_device(text_tokens, images, counts, offsets, norm_gain, value_weight, value_grad):
    sections = lax.axis_size("section")
    columns = lax.axis_size("fsdp")
    pair_count = lax.axis_size("tp")
    tok_rows, feature_width = text_tokens.shape
    img_count, most_slots, feature_slice = images.shape
    group_rows = columns * tok_rows
    pair_index = lax.axis_index("tp")
    column_index = lax.axis_index("fsdp")
    target = offsets // group_rows
    within = offsets % group_rows
    region = within // most_slots
    first_slot = within % most_slots
    section_ids = jnp.arange(sections, dtype=jnp.int32)
    slot_ids = jnp.arange(most_slots, dtype=jnp.int32)
    is_valid = slot_ids[None, :] < counts[:, None]
    placing = (
        (slot_ids[None, :, None] == first_slot[:, None, None] + slot_ids[None, None, :])
        & is_valid[:, None, :]
    ).astype(jnp.bfloat16)
    routing = target[:, None] == section_ids[None, :]
    route_float = routing.astype(jnp.bfloat16)
    route_int = routing.astype(jnp.int32)
    meta_rows = jnp.stack([region, first_slot, counts], axis=1)
    meta_out = jnp.sum(route_int[:, :, None] * meta_rows[:, None, :], axis=0)
    w_rows = collect(value_weight, "fsdp", 0)
    w_own = lax.all_gather(w_rows, "section", axis=1, tiled=True)
    placed = jnp.einsum("krj,kjd->krd", placing, images, preferred_element_type=jnp.float32).astype(
        jnp.bfloat16
    )
    outgoing = jnp.einsum(
        "kt,krd->trd", route_float, placed, preferred_element_type=jnp.float32
    ).astype(jnp.bfloat16)
    arrived, meta_in = (
        lax.all_to_all(outgoing, "section", split_axis=0, concat_axis=0, tiled=True),
        lax.all_to_all(meta_out, "section", split_axis=0, concat_axis=0, tiled=True),
    )
    order_int = (meta_in[:, 0:1] == section_ids[None, :]).astype(jnp.int32)
    order_float = order_int.astype(jnp.bfloat16)
    by_region = jnp.einsum(
        "sr,spd->rpd", order_float, arrived, preferred_element_type=jnp.float32
    ).astype(jnp.bfloat16)
    rows_in = lax.all_to_all(
        by_region.reshape(sections * most_slots, feature_slice),
        "fsdp",
        split_axis=0,
        concat_axis=1,
        tiled=True,
    )
    region_start = jnp.sum(order_int * meta_in[:, 1:2], axis=0)
    region_count = jnp.sum(order_int * meta_in[:, 2:3], axis=0)
    row_ids = column_index * tok_rows + jnp.arange(tok_rows, dtype=jnp.int32)
    row_region = ((row_ids // most_slots)[:, None] == section_ids[None, :]).astype(jnp.int32)
    row_local = row_ids % most_slots
    row_start = jnp.sum(row_region * region_start[None, :], axis=1)
    row_count = jnp.sum(row_region * region_count[None, :], axis=1)
    covered = (row_local >= row_start) & (row_local < row_start + row_count)
    text_own = lax.dynamic_index_in_dim(
        text_tokens.reshape(tok_rows, columns, pair_count, feature_slice),
        pair_index,
        2,
        keepdims=False,
    ).reshape(tok_rows, columns * feature_slice)
    gain_own = lax.dynamic_index_in_dim(
        norm_gain.reshape(columns, pair_count, feature_slice), pair_index, 1, keepdims=False
    ).reshape(-1)
    mixed_rows = jnp.where(covered[:, None], rows_in, text_own)
    mixed_f = mixed_rows.astype(jnp.float32)
    grad_normed = lax.dot_general(
        value_grad, w_own, (((1,), (1,)), ((), ())), preferred_element_type=jnp.float32
    )
    weighted = grad_normed * gain_own
    square_sum, inner_sum = lax.psum(
        (jnp.sum(mixed_f * mixed_f, axis=1), jnp.sum(weighted * mixed_f, axis=1)), "tp"
    )
    inv_rms = lax.rsqrt(square_sum / feature_width + epsilon)[:, None]
    normed = (mixed_f * inv_rms * gain_own).astype(jnp.bfloat16)
    head_part = jnp.dot(normed, w_own, preferred_element_type=jnp.float32)
    values = sent_and_summed(head_part, "tp", 1).astype(jnp.bfloat16)
    grad_own = (
        inv_rms * weighted
        - mixed_f * (inv_rms * inv_rms * inv_rms) * inner_sum[:, None] / feature_width
    ).astype(jnp.bfloat16)
    back_rows = lax.all_to_all(grad_own, "fsdp", split_axis=1, concat_axis=0, tiled=True)
    by_source = jnp.einsum(
        "sr,rpd->spd",
        order_float,
        back_rows.reshape(sections, most_slots, feature_slice),
        preferred_element_type=jnp.float32,
    ).astype(jnp.bfloat16)
    returned = lax.all_to_all(by_source, "section", split_axis=0, concat_axis=0, tiled=True)
    own_rows = jnp.einsum(
        "kt,trd->krd", route_float, returned, preferred_element_type=jnp.float32
    ).astype(jnp.bfloat16)
    visual_grads = jnp.einsum(
        "krj,krd->kjd", placing, own_rows, preferred_element_type=jnp.float32
    ).astype(jnp.bfloat16)
    return (values, visual_grads)


def solution(mesh):
    placed = (
        P(("section", "fsdp"), None),
        P("section", None, ("fsdp", "tp")),
        P("section"),
        P("section"),
        P(),
        P(("fsdp", "tp"), "section"),
        P(("section", "fsdp"), None),
    )
    return jax.shard_map(
        on_device,
        mesh=mesh,
        in_specs=placed,
        out_specs=(P(("section", "fsdp"), "tp"), P("section", None, ("fsdp", "tp"))),
        check_vma=False,
    )
```

profile of v0, /device:TPU:1, one launch (start us, length us, event | category | flops | bytes accessed | tf_op | source)
XLA Modules:
  0.0 399.8 jit_solution(1905969129408803685)
XLA Ops:
  7.2 0.8 fusion.41
  10.1 17.4 %all-to-all-start = ((s32[16,1,3]{2,1,0:T(1,128)}), s32[16,1,3]{2,1,0:T(1,128)S(1)}, u32[]{:S(2)}, u32[]{:S(2)}) async-start(s32[16,1,3]{2,1,0:T(1,128)} %copy.72), calls=%async_computation | async-start | bytes 16384 | tf_op jit(solution)/shard_map/all_to_all | solution.py:70
  28.3 3.0 fusion.17
  31.3 0.8 convolution_convert_fusion.3
  32.4 2.0 all-to-all-done
  34.5 21.8 %all_to_all.67 = bf16[16,256,128]{2,1,0:T(8,128)(2,1)S(1)} all-to-all(bf16[16,256,128]{2,1,0:T(8,128)(2,1)S(1)} %copy.77), channel_id=1, replica_groups=mesh['section'=16,'fsdp'=32,'tp'=2] {'section'}, dimensions={0} | all-to-all | bytes 2097152 | tf_op jit(solution)/shard_map/all_to_all | solution.py:69
  57.1 19.5 %all-to-all-start.3 = ((bf16[32,128,32]{1,2,0:T(8,128)(2,1)}), bf16[32,128,32]{1,2,0:T(8,128)(2,1)S(1)}, u32[]{:S(2)}, u32[]{:S(2)}) async-start(bf16[32,128,32]{1,2,0:T(8,128)(2,1)} %broadcast_in_dim.10), calls=%async_computation.3 | async-start | bytes 524288 | tf_op jit(solution)/shard_map/all_to_all | solution.py:17
  76.6 0.8 convolution_convert_fusion.2
  77.4 1.2 copy.80
  78.7 38.0 %all-to-all-done.3 = bf16[32,128,32]{1,2,0:T(8,128)(2,1)S(1)} async-done(((bf16[32,128,32]{1,2,0:T(8,128)(2,1)}), bf16[32,128,32]{1,2,0:T(8,128)(2,1)S(1)}, u32[]{:S(2)}, u32[]{:S(2)}) %all-to-all-start.3) | async-done | bytes 262176 | tf_op jit(solution)/shard_map/all_to_all | solution.py:17
  116.7 4.2 %all-to-all-start.2 = ((bf16[32,128,128]{2,1,0:T(8,128)(2,1)}), bf16[32,128,128]{2,1,0:T(8,128)(2,1)S(1)}, u32[]{:S(2)}, u32[]{:S(2)}) async-start(bf16[32,128,128]{2,1,0:T(8,128)(2,1)} %bitcast.10), calls=%async_computation.2 | async-start | bytes 2097152 | tf_op jit(solution)/shard_map/all_to_all | solution.py:77
  121.1 0.8 copy_bitcast_fusion.2
  121.9 4.4 %reshape.168 = bf16[128,32,2,128]{3,2,1,0:T(2,128)(2,1)} reshape(bf16[128,8192]{1,0:T(8,128)(2,1)} %param.7) | data formatting | bytes 4194304 | tf_op jit(solution)/shard_map/reshape | solution.py:93
  126.4 9.2 %fusion.42 = (bf16[128,32,128]{2,1,0:T(8,128)(2,1)S(1)}, bf16[128,32,1,128]{3,2,1,0:T(2,128)(2,1)}) fusion(bf16[128,32,2,128]{3,2,1,0:T(2,128)(2,1)} %reshape.168, s32[]{:T(128)S(6)} %select_n.58), kind=kLoop, calls=%fused_computation.83 | loop fusion | bytes 3145732 | tf_op jit(solution)/shard_map/jit(dynamic_index_in_dim)/dynamic_slice | solution.py:92
  135.8 90.2 %all-to-all-done.2 = bf16[32,128,128]{2,1,0:T(8,128)(2,1)S(1)} async-done(((bf16[32,128,128]{2,1,0:T(8,128)(2,1)}), bf16[32,128,128]{2,1,0:T(8,128)(2,1)S(1)}, u32[]{:S(2)}, u32[]{:S(2)}) %all-to-all-start.2) | async-done | bytes 1048608 | tf_op jit(solution)/shard_map/all_to_all | solution.py:77
  226.0 4.1 %fusion.5 = (f32[128]{0:T(128)S(1)}, bf16[128,32,128]{2,0,1:T(8,128)(2,1)}) fusion(bf16[128,32,1,128]{3,2,1,0:T(2,128)(2,1)} %get-tuple-element.9, bf16[32,128,128]{2,1,0:T(8,128)(2,1)S(1)} %all-to-all-done.2, pred[128]{0:T(512)(128)(4,1)S(1)} %compare_and_fusion), kind=kLoop, calls=%fused_computation.9 | loop fusion | flops 2097024 | bytes 3146368 | tf_op jit(solution)/shard_map/reduce_sum | solution.py:108
  230.1 4.7 %fusion.12 = (f32[128]{0:T(128)S(1)}, f32[128,4096]{1,0:T(8,128)}) fusion(bf16[16,8,32,128]{3,2,1,0:T(8,128)(2,1)S(1)} %bitcast.82, pred[128]{0:T(512)(128)(4,1)S(1)} %compare_and_fusion, f32[4096]{0:T(1024)S(1)} %bitcast.86, bf16[128,512]{1,0:T(8,128)(2,1)S(1)} %copy-done.2, bf16[4096,512]{0,1:T(8,128)(2,1)} %all-gather.2.cloned.1.call-done, ...), kind=kOutput, calls=%fused_computation.16 | convolution fusion | flops 539492224 | bytes 8536704 | tf_op jit(solution)/shard_map/dot_general | solution.py:103
  234.8 3.8 all-reduce
  238.5 3.4 copy_bitcast_fusion
  241.9 9.5 %all-to-all-start.5 = ((bf16[128,32,128]{2,0,1:T(8,128)(2,1)}), bf16[128,32,128]{2,0,1:T(8,128)(2,1)S(1)}, u32[]{:S(2)}, u32[]{:S(2)}) async-start(bf16[128,32,128]{2,0,1:T(8,128)(2,1)} %copy_bitcast_fusion), calls=%async_computation.5 | async-start | bytes 2097152 | tf_op jit(solution)/shard_map/all_to_all | solution.py:118
  251.4 1.4 fusion.7
  252.8 1.6 copy.83
  254.4 4.4 %convolution_bitcast_fusion = f32[2,128,256]{2,1,0:T(8,128)} fusion(bf16[128,4096,1]{0,1,2:T(8,128)(2,1)S(1)} %bitcast.85, bf16[2,256,4096]{2,1,0:T(8,128)(2,1)} %bitcast.81), kind=kOutput, calls=%fused_computation.27 | convolution fusion | flops 536870912 | bytes 5505024 | tf_op jit(solution)/shard_map/dot_general | solution.py:112
  258.8 97.7 %all-to-all-done.5 = bf16[128,32,128]{2,0,1:T(8,128)(2,1)S(1)} async-done(((bf16[128,32,128]{2,0,1:T(8,128)(2,1)}), bf16[128,32,128]{2,0,1:T(8,128)(2,1)S(1)}, u32[]{:S(2)}, u32[]{:S(2)}) %all-to-all-start.5) | async-done | bytes 1048608 | tf_op jit(solution)/shard_map/all_to_all | solution.py:118
  356.5 3.4 all-to-all-start.4
  360.0 0.8 convolution_convert_fusion.1
  360.8 1.2 copy.89
  362.0 2.5 all-to-all-done.4
  364.5 7.8 %all-to-all-start.6 = ((bf16[16,256,128]{2,1,0:T(8,128)(2,1)}), bf16[16,256,128]{2,1,0:T(8,128)(2,1)S(1)}, u32[]{:S(2)}, u32[]{:S(2)}) async-start(bf16[16,256,128]{2,1,0:T(8,128)(2,1)} %copy.89), calls=%async_computation.6 | async-start | bytes 2097152 | tf_op jit(solution)/shard_map/all_to_all | solution.py:125
  372.9 16.4 %all-to-all-done.6 = bf16[16,256,128]{2,1,0:T(8,128)(2,1)S(1)} async-done(((bf16[16,256,128]{2,1,0:T(8,128)(2,1)}), bf16[16,256,128]{2,1,0:T(8,128)(2,1)S(1)}, u32[]{:S(2)}, u32[]{:S(2)}) %all-to-all-start.6) | async-done | bytes 1048608 | tf_op jit(solution)/shard_map/all_to_all | solution.py:125
  389.4 0.8 convolution_convert_fusion
  390.1 2.9 fusion.20
  (31 shorter events, 5.2 us)
Async XLA Ops:
  7.2 21.1 %copy-start = (bf16[16,256,128]{2,1,0:T(8,128)(2,1)S(1)}, bf16[16,256,128]{2,1,0:T(8,128)(2,1)}, u32[]{:S(2)}) copy-start(bf16[16,256,128]{2,1,0:T(8,128)(2,1)} %param.8) | copy-start | bytes 3145732
  10.1 24.4 %all-to-all-start = ((s32[16,1,3]{2,1,0:T(1,128)}), s32[16,1,3]{2,1,0:T(1,128)S(1)}, u32[]{:S(2)}, u32[]{:S(2)}) async-start(s32[16,1,3]{2,1,0:T(1,128)} %copy.72), calls=%async_computation | async-start | bytes 16384 | tf_op jit(solution)/shard_map/all_to_all | solution.py:70
  32.2 24.2 %copy-start.3 = (bf16[128,32]{0,1:T(8,128)(2,1)S(1)}, bf16[128,32]{0,1:T(8,128)(2,1)}, u32[]{:S(2)}) copy-start(bf16[128,32]{0,1:T(8,128)(2,1)} %param.12) | copy-start | bytes 24580
  57.1 59.6 %all-to-all-start.3 = ((bf16[32,128,32]{1,2,0:T(8,128)(2,1)}), bf16[32,128,32]{1,2,0:T(8,128)(2,1)S(1)}, u32[]{:S(2)}, u32[]{:S(2)}) async-start(bf16[32,128,32]{1,2,0:T(8,128)(2,1)} %broadcast_in_dim.10), calls=%async_computation.3 | async-start | bytes 524288 | tf_op jit(solution)/shard_map/all_to_all | solution.py:17
  116.7 109.4 %all-to-all-start.2 = ((bf16[32,128,128]{2,1,0:T(8,128)(2,1)}), bf16[32,128,128]{2,1,0:T(8,128)(2,1)S(1)}, u32[]{:S(2)}, u32[]{:S(2)}) async-start(bf16[32,128,128]{2,1,0:T(8,128)(2,1)} %bitcast.10), calls=%async_computation.2 | async-start | bytes 2097152 | tf_op jit(solution)/shard_map/all_to_all | solution.py:77
  120.9 109.2 %all-gather.2.cloned.1.call-start = ((), (), s32[]{:S(2)}) async-start(), calls=%async_computation.7 | async-start | bytes 4456448 | tf_op jit(solution)/shard_map/all_gather | solution.py:61
  121.9 4.5 %copy-start.4 = (f32[8192]{0:T(1024)S(1)}, f32[8192]{0:T(1024)}, u32[]{:S(2)}) copy-start(f32[8192]{0:T(1024)} %param.11) | copy-start | bytes 98308
  226.0 4.1 %copy-start.2 = (bf16[128,512]{1,0:T(8,128)(2,1)S(1)}, bf16[128,512]{1,0:T(8,128)(2,1)}, u32[]{:S(2)}) copy-start(bf16[128,512]{1,0:T(8,128)(2,1)} %param.13) | copy-start | bytes 393220
  241.9 9.5 %copy-start.1 = (bf16[128,32,128]{2,0,1:T(8,128)(2,1)S(1)}, bf16[128,32,128]{2,0,1:T(8,128)(2,1)}, u32[]{:S(2)}) copy-start(bf16[128,32,128]{2,0,1:T(8,128)(2,1)} %get-tuple-element.11) | copy-start | bytes 3145732
  241.9 114.6 %all-to-all-start.5 = ((bf16[128,32,128]{2,0,1:T(8,128)(2,1)}), bf16[128,32,128]{2,0,1:T(8,128)(2,1)S(1)}, u32[]{:S(2)}, u32[]{:S(2)}) async-start(bf16[128,32,128]{2,0,1:T(8,128)(2,1)} %copy_bitcast_fusion), calls=%async_computation.5 | async-start | bytes 2097152 | tf_op jit(solution)/shard_map/all_to_all | solution.py:118
  356.5 7.9 %all-to-all-start.4 = ((f32[2,128,256]{2,1,0:T(8,128)}), f32[2,128,256]{2,1,0:T(8,128)S(1)}, u32[]{:S(2)}, u32[]{:S(2)}) async-start(f32[2,128,256]{2,1,0:T(8,128)} %convolution_bitcast_fusion), calls=%async_computation.4 | async-start | bytes 524288 | tf_op jit(solution)/shard_map/all_to_all | solution.py:31
  364.5 24.9 %all-to-all-start.6 = ((bf16[16,256,128]{2,1,0:T(8,128)(2,1)}), bf16[16,256,128]{2,1,0:T(8,128)(2,1)S(1)}, u32[]{:S(2)}, u32[]{:S(2)}) async-start(bf16[16,256,128]{2,1,0:T(8,128)(2,1)} %copy.89), calls=%async_computation.6 | async-start | bytes 2097152 | tf_op jit(solution)/shard_map/all_to_all | solution.py:125
Sparse Core Ops, SparseCore 0:
  126.2 90.3 all-gather.1
where the time goes:
time: 401 us; the launch traced here: 400 us
  waiting for transfers between devices  247 us (62%)
  starting transfers between devices  62 us (15%)
  blocking collectives  25.6 us (6%)
  local copies, waits for them, and re-layouts  20.3 us (5%)
  matrix products  18.1 us (5%)
  between operations  14.2 us (4%)
  other arithmetic  12.7 us (3%)
    all_to_all x1, waiting for transfers between devices, on_device(): lax.all_to_all(grad_own, 'fsdp', split_axis=1, concat_axis=0, tiled=True)  97.7 us
    all_to_all x1, waiting for transfers between devices, on_device(): lax.all_to_all(by_region.reshape(sections * most_slots, feature_slice), '...  90.2 us
    all_to_all x1, waiting for transfers between devices, sent_to_all(): return lax.all_to_all(copies, axis, split_axis=0, concat_axis=0, tiled=True)  38 us
    all_to_all x1, blocking collectives, on_device(): lax.all_to_all(outgoing, 'section', split_axis=0, concat_axis=0, tiled=True)  21.8 us
    all_to_all x1, starting transfers between devices, sent_to_all(): return lax.all_to_all(copies, axis, split_axis=0, concat_axis=0, tiled=True)  19.5 us
    all_to_all x1, starting transfers between devices, on_device(): lax.all_to_all(meta_out, 'section', split_axis=0, concat_axis=0, tiled=True)  17.4 us
    all_to_all x1, waiting for transfers between devices, on_device(): lax.all_to_all(by_source, 'section', split_axis=0, concat_axis=0, tiled=T...  16.4 us
    all_to_all x1, starting transfers between devices, on_device(): lax.all_to_all(grad_own, 'fsdp', split_axis=1, concat_axis=0, tiled=True)  9.51 us
  transfers between devices with their start and end apart: 7, of which 6 were waited for; matrix products, arithmetic and copies ran while one was open for 9% of the time, Pallas kernels for 0%

commit v1 on v0

v1 whole, which is shorter than its diff:
```python
import jax
import jax.numpy as jnp
from jax import lax
from jax.sharding import PartitionSpec as P


epsilon = 1e-05


def swapped(x, axis, bit):
    length = lax.axis_size(axis)
    return lax.ppermute(x, axis, [(i, i ^ bit) for i in range(length)])


def joined(x, axis, bit):
    other = swapped(x, axis, bit)
    is_high = (lax.axis_index(axis) & bit) != 0
    return jnp.stack([jnp.where(is_high, other, x), jnp.where(is_high, x, other)])


def gathered_by_bits(x, axis):
    length = lax.axis_size(axis)
    rest = x.shape
    bits = length.bit_length() - 1
    for b in range(bits - 1, -1, -1):
        x = joined(x, axis, 1 << b)
    order = tuple(range(bits - 1, -1, -1))
    return x.transpose(order + tuple(range(bits, bits + len(rest)))).reshape(length, *rest)


def on_device(text_tokens, images, counts, offsets, norm_gain, value_weight, value_grad):
    sections = lax.axis_size("section")
    columns = lax.axis_size("fsdp")
    pair_count = lax.axis_size("tp")
    tok_rows, feature_width = text_tokens.shape
    img_count, most_slots, feature_slice = images.shape
    width = value_grad.shape[1]
    half_width = width // pair_count
    half_rows = tok_rows // pair_count
    halves = most_slots // tok_rows
    group_rows = columns * tok_rows
    pair_index = lax.axis_index("tp")
    column_index = lax.axis_index("fsdp")
    plane = ("section", "tp")

    own_half = lax.dynamic_index_in_dim(
        value_grad.reshape(pair_count, half_rows, width), pair_index, 0, keepdims=False
    )
    grads_in = lax.all_gather(own_half, "fsdp", axis=0, tiled=True)

    target = offsets // group_rows
    within = offsets % group_rows
    region = within // most_slots
    first_slot = within % most_slots
    section_ids = jnp.arange(sections, dtype=jnp.int32)
    slot_ids = jnp.arange(most_slots, dtype=jnp.int32)
    is_valid = slot_ids[None, :] < counts[:, None]
    placing = (
        (slot_ids[None, :, None] == first_slot[:, None, None] + slot_ids[None, None, :])
        & is_valid[:, None, :]
    ).astype(jnp.bfloat16)
    routing = target[:, None] == section_ids[None, :]
    route_float = routing.astype(jnp.bfloat16)
    route_int = routing.astype(jnp.int32)
    meta_rows = jnp.stack([region, first_slot, counts], axis=1)
    meta_out = jnp.sum(route_int[:, :, None] * meta_rows[:, None, :], axis=0)
    meta_in = lax.all_to_all(meta_out, "section", split_axis=0, concat_axis=0, tiled=True)

    placed = jnp.einsum("krj,kjd->krd", placing, images, preferred_element_type=jnp.float32).astype(
        jnp.bfloat16
    )
    outgoing = jnp.einsum(
        "kt,krd->trd", route_float, placed, preferred_element_type=jnp.float32
    ).astype(jnp.bfloat16)
    arrived = lax.all_to_all(outgoing, "section", split_axis=0, concat_axis=0, tiled=True)
    order_int = (meta_in[:, 0:1] == section_ids[None, :]).astype(jnp.int32)
    order_float = order_int.astype(jnp.bfloat16)
    by_region = jnp.einsum(
        "sr,spd->rpd", order_float, arrived, preferred_element_type=jnp.float32
    ).astype(jnp.bfloat16)
    rows_in = lax.all_to_all(
        by_region.reshape(columns, tok_rows, feature_slice),
        "fsdp",
        split_axis=0,
        concat_axis=0,
        tiled=True,
    )

    w_start, text_tokens, _ = lax.optimization_barrier((value_weight.T, text_tokens, by_region))
    w_rows = gathered_by_bits(w_start, "fsdp")
    w_all = gathered_by_bits(w_rows.transpose(1, 0, 2), "section")
    w_all = w_all.reshape(width, columns, feature_slice)
    gain_pairs = norm_gain.reshape(columns, pair_count, feature_slice)
    gain_own = lax.dynamic_index_in_dim(gain_pairs, pair_index, 1, keepdims=False)
    w_gain = (w_all.astype(jnp.float32) * gain_own[None]).astype(jnp.bfloat16)
    w_here = lax.dynamic_index_in_dim(w_all, column_index, 1, keepdims=False)
    w_pair = joined(w_here, "tp", 1)
    gain_here = lax.dynamic_index_in_dim(gain_pairs, column_index, 0, keepdims=False)

    region_start = jnp.sum(order_int * meta_in[:, 1:2], axis=0)
    region_count = jnp.sum(order_int * meta_in[:, 2:3], axis=0)
    row_ids = column_index * tok_rows + jnp.arange(tok_rows, dtype=jnp.int32)
    row_region = ((row_ids // most_slots)[:, None] == section_ids[None, :]).astype(jnp.int32)
    row_local = row_ids % most_slots
    row_start = jnp.sum(row_region * region_start[None, :], axis=1)
    row_count = jnp.sum(row_region * region_count[None, :], axis=1)
    covered = (row_local >= row_start) & (row_local < row_start + row_count)

    text_own = lax.dynamic_index_in_dim(
        text_tokens.reshape(tok_rows, columns, pair_count, feature_slice),
        pair_index,
        2,
        keepdims=False,
    )
    text_f = text_own.astype(jnp.float32)
    text_square = jnp.sum(text_f * text_f, axis=(1, 2))
    text_raw = lax.dot_general(
        text_own.reshape(tok_rows, -1),
        w_gain.reshape(width, -1),
        (((1,), (1,)), ((), ())),
        preferred_element_type=jnp.float32,
    )

    rows_f = rows_in.astype(jnp.float32)
    row_square = jnp.sum(rows_f * rows_f, axis=(0, 2))
    row_raw = lax.dot_general(
        rows_in.transpose(1, 0, 2).reshape(tok_rows, -1),
        w_gain.reshape(width, -1),
        (((1,), (1,)), ((), ())),
        preferred_element_type=jnp.float32,
    )
    row_inner = jnp.sum(row_raw * value_grad.astype(jnp.float32), axis=1)

    sums = jnp.stack([row_square, row_inner])
    sums_in = lax.all_to_all(
        jnp.broadcast_to(sums[None], (columns, *sums.shape)), "fsdp", 0, 0, tiled=True
    )
    sums_region = sums_in.reshape(sections, -1)
    order_f32 = order_int.astype(jnp.float32)
    sums_source = jnp.sum(order_f32[:, :, None] * sums_region[None], axis=1)
    sums_both = jnp.broadcast_to(
        sums_source[:, None], (sections, pair_count, sums_source.shape[1])
    ).reshape(sections * pair_count, 8, -1)
    sums_back = lax.all_to_all(sums_both, plane, 0, 0, tiled=True)
    sums_back = jnp.sum(sums_back.reshape(sections, pair_count, -1), axis=1)
    sums_tile = jnp.sum(
        routing.astype(jnp.float32)[:, :, None] * sums_back[None], axis=1
    ).reshape(img_count, halves, 2, tok_rows)
    tile_square = sums_tile[:, :, 0].reshape(img_count, most_slots)
    tile_inner = sums_tile[:, :, 1].reshape(img_count, most_slots)

    raw = jnp.where(covered[:, None], row_raw, text_raw)
    square = jnp.where(covered, row_square, text_square)
    low, high = raw[:, :half_width], raw[:, half_width:]
    is_second = pair_index == 1
    kept = jnp.where(is_second, high, low)
    sent = jnp.where(is_second, low, high)
    lanes = jnp.broadcast_to(square[:, None], (tok_rows, 128))
    got = swapped(jnp.concatenate([sent, lanes], axis=1), "tp", 1)
    full_square = square + got[:, half_width]
    inv_rms = lax.rsqrt(full_square / feature_width + epsilon)[:, None]
    values = ((kept + got[:, :half_width]) * inv_rms).astype(jnp.bfloat16)

    w_pair, _ = lax.optimization_barrier((w_pair, rows_in))
    weighted = jnp.einsum("rn,tnd->rtd", grads_in, w_pair, preferred_element_type=jnp.float32)
    weighted = (weighted * gain_here[None]).astype(jnp.bfloat16)
    weighted = weighted.reshape(sections, halves * half_rows, pair_count, feature_slice)
    by_source = jnp.einsum(
        "sr,rptd->stpd", order_float, weighted, preferred_element_type=jnp.float32
    ).astype(jnp.bfloat16)
    returned = lax.all_to_all(
        by_source.reshape(sections * pair_count, halves * half_rows, feature_slice),
        plane,
        split_axis=0,
        concat_axis=0,
        tiled=True,
    )
    returned = returned.reshape(sections, pair_count, halves, half_rows, feature_slice)
    returned = returned.transpose(0, 2, 1, 3, 4).reshape(sections, most_slots, feature_slice)
    own_weighted = jnp.einsum(
        "kt,trd->krd", route_float, returned, preferred_element_type=jnp.float32
    )
    tile_inv = lax.rsqrt(tile_square / feature_width + epsilon)
    tile_factor = tile_inv * tile_inv * tile_inv * tile_inner / feature_width
    grad_rows = (
        tile_inv[:, :, None] * own_weighted
        - placed.astype(jnp.float32) * tile_factor[:, :, None]
    ).astype(jnp.bfloat16)
    visual_grads = jnp.einsum(
        "krj,krd->kjd", placing, grad_rows, preferred_element_type=jnp.float32
    ).astype(jnp.bfloat16)
    return (values, visual_grads)


def solution(mesh):
    placed = (
        P(("section", "fsdp"), None),
        P("section", None, ("fsdp", "tp")),
        P("section"),
        P("section"),
        P(),
        P(("fsdp", "tp"), "section"),
        P(("section", "fsdp"), None),
    )

    return jax.shard_map(
        on_device,
        mesh=mesh,
        in_specs=placed,
        out_specs=(P(("section", "fsdp"), "tp"), P("section", None, ("fsdp", "tp"))),
        check_vma=False,
    )
```

time: 401 us -> 466 us (1.16)
  starting transfers between devices: 62 us -> 165 us
  blocking collectives: 25.6 us -> 0 us
  waiting for transfers between devices: 247 us -> 224 us
  other arithmetic: 12.7 us -> 18.4 us
    all_to_all x5, waiting for transfers between devices: 245 us -> 35 us  [the longest x1 17 us: on_device(): lax.all_to_all(outgoing, 'section', split_axis=0, concat_axis=0, tiled=True)]
    ppermute x0 -> x11, waiting for transfers between devices: none -> 131 us  [swapped(): return lax.ppermute(x, axis, [(i, i ^ bit) for i in range(length)])]
    ppermute x0 -> x11, starting transfers between devices: none -> 61.7 us  [swapped(): return lax.ppermute(x, axis, [(i, i ^ bit) for i in range(length)])]
    all_gather x1, waiting for transfers between devices: 0.01 us -> 58.4 us  [on_device(): grads_in = lax.all_gather(own_half, 'fsdp', axis=0, tiled=True)]
    all_to_all x5, starting transfers between devices: 44.4 us -> 85.6 us  [the longest x1 27.7 us: on_device(): sums_back = lax.all_to_all(sums_both, plane, 0, 0, tiled=True)]
    all_to_all x1 -> x0, blocking collectives: 21.8 us -> none  [on_device(): lax.all_to_all(outgoing, 'section', split_axis=0, concat_axis=0, tiled=True)]
    dynamic_slice x2 -> x3, local copies, waits for them, and re-layouts: 9.22 us -> 0.94 us  [the longest x1 0.64 us: on_device(): lax.dynamic_index_in_dim(value_grad.reshape(pair_count, half_rows, width)...]
    another operation x0 -> x20, other arithmetic: none -> 5.5 us  [the longest x19 5.49 us: joined(): jnp.stack([jnp.where(is_high, other, x), jnp.where(is_high, x, other)])]
  transfers between devices with their start and end apart: 7 -> 18, of which waited for: 6 -> 12; matrix products, arithmetic and copies ran while one was open for 9% -> 11% of each run, Pallas kernels for 0% -> 0%
where the time goes in v1:
time: 466 us; the launch traced here: 465 us
  waiting for transfers between devices  224 us (48%)
  starting transfers between devices  165 us (35%)
  matrix products  22 us (5%)
  local copies, waits for them, and re-layouts  20.8 us (4%)
  other arithmetic  18.4 us (4%)
  between operations  14.7 us (3%)
    ppermute x11, waiting for transfers between devices, swapped(): return lax.ppermute(x, axis, [(i, i ^ bit) for i in range(length)])  131 us
    ppermute x11, starting transfers between devices, swapped(): return lax.ppermute(x, axis, [(i, i ^ bit) for i in range(length)])  61.7 us
    all_gather x1, waiting for transfers between devices, on_device(): grads_in = lax.all_gather(own_half, 'fsdp', axis=0, tiled=True)  58.4 us
    all_to_all x1, starting transfers between devices, on_device(): sums_back = lax.all_to_all(sums_both, plane, 0, 0, tiled=True)  27.7 us
    all_to_all x1, starting transfers between devices, on_device(): lax.all_to_all(jnp.broadcast_to(sums[None], (columns, *sums.shape)), 'fsd...  25.9 us
    all_to_all x1, starting transfers between devices, on_device(): lax.all_to_all(by_region.reshape(columns, tok_rows, feature_slice), 'fsdp...  20.4 us
    all_to_all x1, starting transfers between devices, on_device(): lax.all_to_all(meta_out, 'section', split_axis=0, concat_axis=0, tiled=True)  17.4 us
    all_to_all x1, waiting for transfers between devices, on_device(): lax.all_to_all(outgoing, 'section', split_axis=0, concat_axis=0, tiled=True)  17 us
  transfers between devices with their start and end apart: 18, of which 12 were waited for; matrix products, arithmetic and copies ran while one was open for 11% of the time, Pallas kernels for 0%

profile of v1, /device:TPU:1, one launch (start us, length us, event | category | flops | bytes accessed | tf_op | source)
XLA Modules:
  0.0 464.7 jit_solution(10684528106294497358)
XLA Ops:
  9.5 17.4 %all-to-all-start = ((s32[16,1,3]{2,1,0:T(1,128)}), s32[16,1,3]{2,1,0:T(1,128)S(1)}, u32[]{:S(2)}, u32[]{:S(2)}) async-start(s32[16,1,3]{2,1,0:T(1,128)} %copy.170), calls=%async_computation | async-start | bytes 16384 | tf_op jit(solution)/shard_map/all_to_all | solution.py:67
  27.7 3.0 fusion.18
  33.8 7.3 %all-to-all-start.1 = ((bf16[16,256,128]{2,1,0:T(8,128)(2,1)}), bf16[16,256,128]{2,1,0:T(8,128)(2,1)S(1)}, u32[]{:S(2)}, u32[]{:S(2)}) async-start(bf16[16,256,128]{2,1,0:T(8,128)(2,1)} %copy.175), calls=%async_computation.1 | async-start | bytes 2097152 | tf_op jit(solution)/shard_map/all_to_all | solution.py:75
  41.3 17.0 %all-to-all-done.1 = bf16[16,256,128]{2,1,0:T(8,128)(2,1)S(1)} async-done(((bf16[16,256,128]{2,1,0:T(8,128)(2,1)}), bf16[16,256,128]{2,1,0:T(8,128)(2,1)S(1)}, u32[]{:S(2)}, u32[]{:S(2)}) %all-to-all-start.1) | async-done | bytes 1048608 | tf_op jit(solution)/shard_map/all_to_all | solution.py:75
  59.1 19.7 %collective-permute-start = (bf16[32,128]{1,0:T(8,128)(2,1)S(1)}, bf16[32,128]{1,0:T(8,128)(2,1)S(1)}, u32[]{:S(2)}, u32[]{:S(2)}) collective-permute-start(bf16[32,128]{1,0:T(8,128)(2,1)S(1)} %bitcast.181), channel_id=1, source_target_pairs={{0,32},{2,34},{4,36},{6,38},{8,40},{10,42},{12,44},{14,46},{16,48}... | collective-permute-start | bytes 24584 | tf_op jit(solution)/shard_map/ppermute | solution.py:12
  78.8 3.0 collective-permute-done
  81.8 6.4 %collective-permute-start.1 = (bf16[2,32,128]{2,1,0:T(8,128)(2,1)S(1)}, bf16[2,32,128]{2,1,0:T(8,128)(2,1)S(1)}, u32[]{:S(2)}, u32[]{:S(2)}) collective-permute-start(bf16[2,32,128]{2,1,0:T(8,128)(2,1)S(1)} %pad_maximum_fusion.9), channel_id=1, source_target_pairs={{0,16},{2,18},{4,20},{6,22},{8,24},{10,26},{12,28},{14,30},{16,0},... | collective-permute-start | bytes 49160 | tf_op jit(solution)/shard_map/ppermute | solution.py:12
  88.3 6.7 %collective-permute-done.1 = bf16[2,32,128]{2,1,0:T(8,128)(2,1)S(1)} collective-permute-done((bf16[2,32,128]{2,1,0:T(8,128)(2,1)S(1)}, bf16[2,32,128]{2,1,0:T(8,128)(2,1)S(1)}, u32[]{:S(2)}, u32[]{:S(2)}) %collective-permute-start.1) | collective-permute-done | bytes 16416 | tf_op jit(solution)/shard_map/ppermute | solution.py:12
  95.0 3.2 collective-permute-start.2
  99.5 20.4 %all-to-all-start.2 = ((bf16[32,128,128]{2,1,0:T(8,128)(2,1)}), bf16[32,128,128]{2,1,0:T(8,128)(2,1)}, u32[]{:S(2)}, u32[]{:S(2)}) async-start(bf16[32,128,128]{2,1,0:T(8,128)(2,1)} %bitcast.10), calls=%async_computation.2 | async-start | bytes 2097152 | tf_op jit(solution)/shard_map/all_to_all | solution.py:81
  120.0 4.0 collective-permute-start.3
  124.0 84.5 %collective-permute-done.3 = bf16[2,2,2,32,128]{4,3,0,1,2:T(8,128)(2,1)S(1)} collective-permute-done((bf16[2,2,2,32,128]{4,3,0,1,2:T(8,128)(2,1)S(1)}, bf16[2,2,2,32,128]{4,3,0,1,2:T(8,128)(2,1)S(1)}, u32[]{:S(2)}, u32[]{:S(2)}) %collective-permute-start.3) | collective-permute-done | bytes 65568 | tf_op jit(solution)/shard_map/ppermute | solution.py:12
  208.5 5.2 %collective-permute-start.4 = (bf16[2,2,2,2,32,128]{5,4,0,1,2,3:T(8,128)(2,1)S(1)}, bf16[2,2,2,2,32,128]{5,4,0,1,2,3:T(8,128)(2,1)S(1)}, u32[]{:S(2)}, u32[]{:S(2)}) collective-permute-start(bf16[2,2,2,2,32,128]{5,4,0,1,2,3:T(8,128)(2,1)S(1)} %pad_maximum_fusion.6), channel_id=1, source_target_pairs={{0,2},{2,0},{4,6},{6,4},{8,10},{10,8},{12,14},{14,12},{16,18},{18,... | collective-permute-start | bytes 393224 | tf_op jit(solution)/shard_map/ppermute | solution.py:12
  213.7 3.1 collective-permute-done.4
  219.3 6.5 %collective-permute-done.5 = bf16[32,32,128]{2,0,1:T(8,128)(2,1)S(1)} collective-permute-done((bf16[32,32,128]{2,0,1:T(8,128)(2,1)S(1)}, bf16[32,32,128]{2,0,1:T(8,128)(2,1)S(1)}, u32[]{:S(2)}, u32[]{:S(2)}) %collective-permute-start.5) | collective-permute-done | bytes 262176 | tf_op jit(solution)/shard_map/ppermute | solution.py:12
  227.9 8.7 %collective-permute-done.6 = bf16[2,32,32,128]{3,1,2,0:T(8,128)(2,1)S(1)} collective-permute-done((bf16[2,32,32,128]{3,1,2,0:T(8,128)(2,1)S(1)}, bf16[2,32,32,128]{3,1,2,0:T(8,128)(2,1)S(1)}, u32[]{:S(2)}, u32[]{:S(2)}) %collective-permute-start.6) | collective-permute-done | bytes 524320 | tf_op jit(solution)/shard_map/ppermute | solution.py:12
  237.7 5.3 %collective-permute-start.7 = (bf16[2,2,32,32,128]{4,2,3,1,0:T(8,128)(2,1)S(1)}, bf16[2,2,32,32,128]{4,2,3,1,0:T(8,128)(2,1)}, u32[]{:S(2)}, u32[]{:S(2)}) collective-permute-start(bf16[2,2,32,32,128]{4,2,3,1,0:T(8,128)(2,1)S(1)} %pad_maximum_fusion.1), channel_id=1, source_target_pairs={{0,128},{64,192},{128,0},{192,64},{256,384},{320,448},{384,256},{4... | collective-permute-start | bytes 3145736 | tf_op jit(solution)/shard_map/ppermute | solution.py:12
  243.0 18.2 %collective-permute-done.7 = bf16[2,2,32,32,128]{4,2,3,1,0:T(8,128)(2,1)} collective-permute-done((bf16[2,2,32,32,128]{4,2,3,1,0:T(8,128)(2,1)S(1)}, bf16[2,2,32,32,128]{4,2,3,1,0:T(8,128)(2,1)}, u32[]{:S(2)}, u32[]{:S(2)}) %collective-permute-start.7) | collective-permute-done | bytes 1048608 | tf_op jit(solution)/shard_map/ppermute | solution.py:12
  264.5 7.9 %collective-permute-start.8 = (bf16[2,2,2,32,32,128]{5,3,4,2,1,0:T(8,128)(2,1)}, bf16[2,2,2,32,32,128]{5,3,4,2,1,0:T(8,128)(2,1)}, u32[]{:S(2)}, u32[]{:S(2)}) collective-permute-start(bf16[2,2,2,32,32,128]{5,3,4,2,1,0:T(8,128)(2,1)} %pad_maximum_fusion), channel_id=1, source_target_pairs={{0,64},{64,0},{128,192},{192,128},{256,320},{320,256},{384,448},{4... | collective-permute-start | bytes 6291464 | tf_op jit(solution)/shard_map/ppermute | solution.py:12
  273.3 4.1 copy.185
  287.0 3.1 multiply_convert_fusion.1
  291.2 3.7 copy.186
  296.5 5.0 %multiply_reduce_fusion.4 = (f32[128]{0:T(128)S(1)}, f32[128,512]{1,0:T(8,128)S(1)}) fusion(bf16[128,512]{1,0:T(8,128)(2,1)S(1)} %copy-done.6, bf16[512,32,128]{2,1,0:T(8,128)(2,1)} %multiply_convert_fusion.1, bf16[32,128,128]{2,1,0:T(8,128)(2,1)} %all-to-all-done.2), kind=kOutput, calls=%fused_computation.53 | convolution fusion | flops 537067392 | bytes 5636608 | tf_op jit(solution)/shard_map/dot_general | solution.py:126
  302.1 25.9 %all-to-all-start.3 = ((f32[32,2,128]{2,1,0:T(2,128)}), f32[32,2,128]{2,1,0:T(2,128)S(1)}, u32[]{:S(2)}, u32[]{:S(2)}) async-start(f32[32,2,128]{2,1,0:T(2,128)} %broadcast_in_dim.13), calls=%async_computation.3 | async-start | bytes 65536 | tf_op jit(solution)/shard_map/all_to_all | solution.py:135
  328.2 3.5 fusion.28
  331.8 3.1 collective-permute-start.9
  334.9 58.4 %all-gather.3.cloned.1.call-done = bf16[1,2048,512]{2,1,0:T(8,128)(2,1)} async-done(((bf16[1,64,512]{2,1,0:T(8,128)(2,1)}), bf16[1,2048,512]{2,1,0:T(8,128)(2,1)}) %all-gather.3.cloned.1.call-update) | async-done | bytes 2097168 | tf_op jit(solution)/shard_map/all_gather | solution.py:49
  396.7 27.7 %all-to-all-start.4 = ((f32[32,1,512]{2,1,0:T(1,128)}), f32[32,1,512]{2,1,0:T(1,128)S(1)}, u32[]{:S(2)}, u32[]{:S(2)}) async-start(f32[32,1,512]{2,1,0:T(1,128)} %reshape.326), calls=%async_computation.4 | async-start | bytes 131072 | tf_op jit(solution)/shard_map/all_to_all | solution.py:144
  426.6 4.9 %all-to-all-done.4 = f32[32,1,512]{2,1,0:T(1,128)S(1)} async-done(((f32[32,1,512]{2,1,0:T(1,128)}), f32[32,1,512]{2,1,0:T(1,128)S(1)}, u32[]{:S(2)}, u32[]{:S(2)}) %all-to-all-start.4) | async-done | bytes 65568 | tf_op jit(solution)/shard_map/all_to_all | solution.py:144
  431.5 4.4 all-to-all-start.5
  438.5 13.1 %all-to-all-done.5 = bf16[32,128,128]{2,1,0:T(8,128)(2,1)S(1)} async-done(((bf16[32,128,128]{2,1,0:T(8,128)(2,1)}), bf16[32,128,128]{2,1,0:T(8,128)(2,1)S(1)}, u32[]{:S(2)}, u32[]{:S(2)}) %all-to-all-start.5) | async-done | bytes 1048608 | tf_op jit(solution)/shard_map/all_to_all | solution.py:171
  452.9 5.0 %fusion.21 = bf16[16,256,128]{2,1,0:T(8,128)(2,1)} fusion(s32[16,256]{1,0:T(8,128)S(1)} %iota_add_fusion, pred[16,256]{1,0:T(8,128)(4,1)S(1)} %iota_compare_fusion.1, f32[16,256,128]{2,0,1:T(8,128)S(1)} %fusion.33, bf16[16,256,128]{2,1,0:T(8,128)(2,1)S(1)} %copy-done.4, f32[16,256]{1,0:T(8,128)S(1)} %fusion.43, f32[16,256]{1,0:T(8,128)S(1)} %bitcast.176), kind=kOutput, calls=%fused_computation.28 | convolution fusion | flops 273678336 | bytes 4247552 | tf_op jit(solution)/shard_map/krj,krd->kjd/dot_general | solution.py:189
  (109 shorter events, 40.8 us)
Async XLA Ops:
  7.2 20.5 %copy-start = (bf16[16,256,128]{2,1,0:T(8,128)(2,1)S(1)}, bf16[16,256,128]{2,1,0:T(8,128)(2,1)}, u32[]{:S(2)}) copy-start(bf16[16,256,128]{2,1,0:T(8,128)(2,1)} %param.8) | copy-start | bytes 3145732
  9.5 24.4 %all-to-all-start = ((s32[16,1,3]{2,1,0:T(1,128)}), s32[16,1,3]{2,1,0:T(1,128)S(1)}, u32[]{:S(2)}, u32[]{:S(2)}) async-start(s32[16,1,3]{2,1,0:T(1,128)} %copy.170), calls=%async_computation | async-start | bytes 16384 | tf_op jit(solution)/shard_map/all_to_all | solution.py:67
  30.7 1.0 copy-start.3
  33.7 25.3 %copy-start.8 = (bf16[128,32]{0,1:T(8,128)(2,1)S(1)}, bf16[128,32]{0,1:T(8,128)(2,1)}, u32[]{:S(2)}) copy-start(bf16[128,32]{0,1:T(8,128)(2,1)} %param.12) | copy-start | bytes 24580
  33.8 24.4 %all-to-all-start.1 = ((bf16[16,256,128]{2,1,0:T(8,128)(2,1)}), bf16[16,256,128]{2,1,0:T(8,128)(2,1)S(1)}, u32[]{:S(2)}, u32[]{:S(2)}) async-start(bf16[16,256,128]{2,1,0:T(8,128)(2,1)} %copy.175), calls=%async_computation.1 | async-start | bytes 2097152 | tf_op jit(solution)/shard_map/all_to_all | solution.py:75
  59.1 22.7 %collective-permute-start = (bf16[32,128]{1,0:T(8,128)(2,1)S(1)}, bf16[32,128]{1,0:T(8,128)(2,1)S(1)}, u32[]{:S(2)}, u32[]{:S(2)}) collective-permute-start(bf16[32,128]{1,0:T(8,128)(2,1)S(1)} %bitcast.181), channel_id=1, source_target_pairs={{0,32},{2,34},{4,36},{6,38},{8,40},{10,42},{12,44},{14,46},{16,48}... | collective-permute-start | bytes 24584 | tf_op jit(solution)/shard_map/ppermute | solution.py:12
  81.8 13.2 %collective-permute-start.1 = (bf16[2,32,128]{2,1,0:T(8,128)(2,1)S(1)}, bf16[2,32,128]{2,1,0:T(8,128)(2,1)S(1)}, u32[]{:S(2)}, u32[]{:S(2)}) collective-permute-start(bf16[2,32,128]{2,1,0:T(8,128)(2,1)S(1)} %pad_maximum_fusion.9), channel_id=1, source_target_pairs={{0,16},{2,18},{4,20},{6,22},{8,24},{10,26},{12,28},{14,30},{16,0},... | collective-permute-start | bytes 49160 | tf_op jit(solution)/shard_map/ppermute | solution.py:12
  95.0 24.9 %collective-permute-start.2 = (bf16[2,2,32,128]{3,2,0,1:T(8,128)(2,1)S(1)}, bf16[2,2,32,128]{3,2,0,1:T(8,128)(2,1)S(1)}, u32[]{:S(2)}, u32[]{:S(2)}) collective-permute-start(bf16[2,2,32,128]{3,2,0,1:T(8,128)(2,1)S(1)} %pad_maximum_fusion.8), channel_id=1, source_target_pairs={{0,8},{2,10},{4,12},{6,14},{8,0},{10,2},{12,4},{14,6},{16,24},{18,... | collective-permute-start | bytes 98312 | tf_op jit(solution)/shard_map/ppermute | solution.py:12
  99.5 195.4 %all-to-all-start.2 = ((bf16[32,128,128]{2,1,0:T(8,128)(2,1)}), bf16[32,128,128]{2,1,0:T(8,128)(2,1)}, u32[]{:S(2)}, u32[]{:S(2)}) async-start(bf16[32,128,128]{2,1,0:T(8,128)(2,1)} %bitcast.10), calls=%async_computation.2 | async-start | bytes 2097152 | tf_op jit(solution)/shard_map/all_to_all | solution.py:81
  119.9 273.4 %all-gather.3.cloned.1.call-start = ((), (), s32[]{:S(2)}) async-start(), calls=%async_computation.6 | async-start | bytes 2162688 | tf_op jit(solution)/shard_map/all_gather | solution.py:49
  120.0 88.4 %collective-permute-start.3 = (bf16[2,2,2,32,128]{4,3,0,1,2:T(8,128)(2,1)S(1)}, bf16[2,2,2,32,128]{4,3,0,1,2:T(8,128)(2,1)S(1)}, u32[]{:S(2)}, u32[]{:S(2)}) collective-permute-start(bf16[2,2,2,32,128]{4,3,0,1,2:T(8,128)(2,1)S(1)} %pad_maximum_fusion.7), channel_id=1, source_target_pairs={{0,4},{2,6},{4,0},{6,2},{8,12},{10,14},{12,8},{14,10},{16,20},{18,... | collective-permute-start | bytes 196616 | tf_op jit(solution)/shard_map/ppermute | solution.py:12
  208.5 8.3 %collective-permute-start.4 = (bf16[2,2,2,2,32,128]{5,4,0,1,2,3:T(8,128)(2,1)S(1)}, bf16[2,2,2,2,32,128]{5,4,0,1,2,3:T(8,128)(2,1)S(1)}, u32[]{:S(2)}, u32[]{:S(2)}) collective-permute-start(bf16[2,2,2,2,32,128]{5,4,0,1,2,3:T(8,128)(2,1)S(1)} %pad_maximum_fusion.6), channel_id=1, source_target_pairs={{0,2},{2,0},{4,6},{6,4},{8,10},{10,8},{12,14},{14,12},{16,18},{18,... | collective-permute-start | bytes 393224 | tf_op jit(solution)/shard_map/ppermute | solution.py:12
  216.8 9.0 %collective-permute-start.5 = (bf16[32,32,128]{2,0,1:T(8,128)(2,1)S(1)}, bf16[32,32,128]{2,0,1:T(8,128)(2,1)S(1)}, u32[]{:S(2)}, u32[]{:S(2)}) collective-permute-start(bf16[32,32,128]{2,0,1:T(8,128)(2,1)S(1)} %bitcast.168), channel_id=1, source_target_pairs={{0,512},{64,576},{128,640},{192,704},{256,768},{320,832},{384,896}... | collective-permute-start | bytes 786440 | tf_op jit(solution)/shard_map/ppermute | solution.py:12
  226.0 10.7 %collective-permute-start.6 = (bf16[2,32,32,128]{3,1,2,0:T(8,128)(2,1)S(1)}, bf16[2,32,32,128]{3,1,2,0:T(8,128)(2,1)S(1)}, u32[]{:S(2)}, u32[]{:S(2)}) collective-permute-start(bf16[2,32,32,128]{3,1,2,0:T(8,128)(2,1)S(1)} %pad_maximum_fusion.2), channel_id=1, source_target_pairs={{0,256},{64,320},{128,384},{192,448},{256,0},{320,64},{384,128},{4... | collective-permute-start | bytes 1572872 | tf_op jit(solution)/shard_map/ppermute | solution.py:12
  236.7 0.8 copy-start.1
  236.7 1.0 copy-start.2
  237.7 23.5 %collective-permute-start.7 = (bf16[2,2,32,32,128]{4,2,3,1,0:T(8,128)(2,1)S(1)}, bf16[2,2,32,32,128]{4,2,3,1,0:T(8,128)(2,1)}, u32[]{:S(2)}, u32[]{:S(2)}) collective-permute-start(bf16[2,2,32,32,128]{4,2,3,1,0:T(8,128)(2,1)S(1)} %pad_maximum_fusion.1), channel_id=1, source_target_pairs={{0,128},{64,192},{128,0},{192,64},{256,384},{320,448},{384,256},{4... | collective-permute-start | bytes 3145736 | tf_op jit(solution)/shard_map/ppermute | solution.py:12
  262.9 9.4 %copy-start.6 = (bf16[128,512]{1,0:T(8,128)(2,1)S(1)}, bf16[128,512]{1,0:T(8,128)(2,1)}, u32[]{:S(2)}) copy-start(bf16[128,512]{1,0:T(8,128)(2,1)} %param.13) | copy-start | bytes 393220
  262.9 10.1 %copy-start.7 = (f32[8192]{0:T(1024)S(1)}, f32[8192]{0:T(1024)}, u32[]{:S(2)}) copy-start(f32[8192]{0:T(1024)} %param.11) | copy-start | bytes 98308
  264.5 15.7 %collective-permute-start.8 = (bf16[2,2,2,32,32,128]{5,3,4,2,1,0:T(8,128)(2,1)}, bf16[2,2,2,32,32,128]{5,3,4,2,1,0:T(8,128)(2,1)}, u32[]{:S(2)}, u32[]{:S(2)}) collective-permute-start(bf16[2,2,2,32,32,128]{5,3,4,2,1,0:T(8,128)(2,1)} %pad_maximum_fusion), channel_id=1, source_target_pairs={{0,64},{64,0},{128,192},{192,128},{256,320},{320,256},{384,448},{4... | collective-permute-start | bytes 6291464 | tf_op jit(solution)/shard_map/ppermute | solution.py:12
  284.5 10.3 %collective-permute-start.10 = (bf16[512,128]{1,0:T(8,128)(2,1)S(1)}, bf16[512,128]{1,0:T(8,128)(2,1)S(1)}, u32[]{:S(2)}, u32[]{:S(2)}) collective-permute-start(bf16[512,128]{1,0:T(8,128)(2,1)S(1)} %bitcast.173), channel_id=1, source_target_pairs={{0,1},{1,0},{2,3},{3,2},{4,5},{5,4},{6,7},{7,6},{8,9},{9,8},{10,11... | collective-permute-start | bytes 393224 | tf_op jit(solution)/shard_map/ppermute | solution.py:12
  296.5 31.8 %copy-start.5 = (bf16[128,32,1,128]{0,3,2,1:T(8,128)(2,1)S(1)}, bf16[128,32,1,128]{0,3,2,1:T(8,128)(2,1)}, u32[]{:S(2)}) copy-start(bf16[128,32,1,128]{0,3,2,1:T(8,128)(2,1)} %get-tuple-element.19) | copy-start | bytes 3145732
  302.1 93.5 %all-to-all-start.3 = ((f32[32,2,128]{2,1,0:T(2,128)}), f32[32,2,128]{2,1,0:T(2,128)S(1)}, u32[]{:S(2)}, u32[]{:S(2)}) async-start(f32[32,2,128]{2,1,0:T(2,128)} %broadcast_in_dim.13), calls=%async_computation.3 | async-start | bytes 65536 | tf_op jit(solution)/shard_map/all_to_all | solution.py:135
  331.8 104.1 %collective-permute-start.9 = (f32[128,384]{0,1:T(8,128)S(1)}, f32[128,384]{0,1:T(8,128)S(1)}, u32[]{:S(2)}, u32[]{:S(2)}) collective-permute-start(f32[128,384]{0,1:T(8,128)S(1)} %pad_maximum_fusion.5), channel_id=1, source_target_pairs={{0,1},{1,0},{2,3},{3,2},{4,5},{5,4},{6,7},{7,6},{8,9},{9,8},{10,11... | collective-permute-start | bytes 589832 | tf_op jit(solution)/shard_map/ppermute | solution.py:12
  396.7 34.7 %all-to-all-start.4 = ((f32[32,1,512]{2,1,0:T(1,128)}), f32[32,1,512]{2,1,0:T(1,128)S(1)}, u32[]{:S(2)}, u32[]{:S(2)}) async-start(f32[32,1,512]{2,1,0:T(1,128)} %reshape.326), calls=%async_computation.4 | async-start | bytes 131072 | tf_op jit(solution)/shard_map/all_to_all | solution.py:144
  431.5 20.1 %all-to-all-start.5 = ((bf16[32,128,128]{2,1,0:T(8,128)(2,1)}), bf16[32,128,128]{2,1,0:T(8,128)(2,1)S(1)}, u32[]{:S(2)}, u32[]{:S(2)}) async-start(bf16[32,128,128]{2,1,0:T(8,128)(2,1)} %bitcast.65), calls=%async_computation.5 | async-start | bytes 2097152 | tf_op jit(solution)/shard_map/all_to_all | solution.py:171
  451.7 1.2 copy-start.4
Sparse Core Ops, SparseCore 0:
  273.1 120.1 all-gather.2
